TPU v7x, 32 devices: a whole 2x2x4 slice. The times are simulated.
32 devices in a mesh: dp: 16 (over z, x, core), tensor: 2 (over y).
Axes of the slice: x: 2, y: 2, z: 4, core: 2. Of those that a mesh axis runs over, the one named last changes fastest.
Arguments:
- layer_input: bfloat16 [2, 8192, 1024], P(None, ('dp', 'tensor')), may hold values from -6 to 6
- segment_ids: int32 [2, 8192], P(None, 'dp'), may hold values from 0 to 5, as said below
- qkv_weight: bfloat16 [3, 1024, 1024], P(None, 'dp', 'tensor'), may hold values from -0.1875 to 0.1875
- qv_bias: bfloat16 [2, 16, 64], P(None, 'tensor', 'dp'), may hold values from -3 to 3
- out_weight: bfloat16 [1024, 1024], P('tensor', 'dp'), may hold values from -1 to 1
- up_weight: bfloat16 [1024, 4096], P('dp', 'tensor'), may hold values from -0.1875 to 0.1875
- up_bias: bfloat16 [2, 2048], P('tensor', 'dp'), may hold values from -3 to 3
- down_weight: bfloat16 [4096, 1024], P('tensor', 'dp'), may hold values from -0.09375 to 0.09375
- norm_gains: float32 [2, 1024], P(None, ('dp', 'tensor')), may hold values from 0.1 to 1.9
- row_biases: float32 [4, 1024], P(None, ('dp', 'tensor')), may hold values from -2 to 2
- cotangent: bfloat16 [2, 8192, 1024], P(None, ('dp', 'tensor')), may hold values from -6 to 6
Outputs:
- layer_output: bfloat16 [2, 8192, 1024], P(None, ('dp', 'tensor'))
- input_grad: bfloat16 [2, 8192, 1024], P(None, ('dp', 'tensor'))
- qkv_weight_grad: float32 [3, 1024, 1024], P(None, 'dp', 'tensor')
- qv_bias_grad: float32 [2, 16, 64], P(None, 'tensor', 'dp')
- out_weight_grad: float32 [1024, 1024], P('tensor', 'dp')
- up_weight_grad: float32 [1024, 4096], P('dp', 'tensor')
- up_bias_grad: float32 [2, 2048], P('tensor', 'dp')
- down_weight_grad: float32 [4096, 1024], P('tensor', 'dp')
- norm_gains_grad: float32 [2, 1024], P(None, ('dp', 'tensor'))
- row_biases_grad: float32 [4, 1024], P(None, ('dp', 'tensor'))
Inputs may be any that keep to these rules, and one draw needn't show every extreme that they name: `segment_ids`: within every sequence of 512 rows, documents 1 to 5 follow one another in order, each 20 to 100 tokens long, and padding with id 0 fills the rest, 12 tokens or more.
All inputs are finite; a program needn't handle non-finite values.
Results may differ from a plain program's by a relative error of at most 0.02.
Values may be sent and summed in bfloat16 or wider, within the bound.
No kernel may reach another device: no remote copies, remote signals or barrier semaphores. Data moves between devices by JAX's collectives and lax.ppermute only.
A program may use at most 192 MiB of HBM per device.

v0:
```python
import jax
import jax.numpy as jnp
from jax import lax
from jax.sharding import PartitionSpec as P

HEAD_DIM = 64


def gelu_exact(values):
    return jax.nn.gelu(values, approximate=False)


def normalize(rows, gain, shift):
    centered = rows - jnp.mean(rows, axis=-1, keepdims=True)
    variance = jnp.mean(centered * centered, axis=-1, keepdims=True)
    inverse = lax.rsqrt(variance + 1e-05)
    normed = centered * inverse
    return (normed * gain + shift, normed, inverse)


def norm_back(grad, normed, inverse, gain):
    scaled = grad * gain
    return inverse * (
        scaled
        - jnp.mean(scaled, axis=-1, keepdims=True)
        - normed * jnp.mean(scaled * normed, axis=-1, keepdims=True)
    )


def attend(query, keys, values, keep_mask, scale):
    scores = jnp.einsum("qhd,khd->hqk", query, keys, preferred_element_type=jnp.float32) * scale
    masked = jnp.where(keep_mask[None], scores, -1e30)
    highest = jnp.max(masked, axis=-1, keepdims=True)
    shifted = jnp.exp(masked - highest)
    totals = jnp.sum(shifted, axis=-1, keepdims=True)
    probs = (shifted / totals).astype(jnp.bfloat16)
    context = jnp.einsum("hqk,khd->qhd", probs, values, preferred_element_type=jnp.float32)
    return (context, highest + jnp.log(totals))


def attend_back(query, keys, values, keep_mask, logsumexp, grad_context, scale):
    scores = jnp.einsum("qhd,khd->hqk", query, keys, preferred_element_type=jnp.float32) * scale
    masked = jnp.where(keep_mask[None], scores, -1e30)
    probs = jnp.exp(masked - logsumexp)
    probs_low = probs.astype(jnp.bfloat16)
    grad_values = jnp.einsum(
        "hqk,qhd->khd", probs_low, grad_context, preferred_element_type=jnp.float32
    )
    grad_probs = jnp.einsum(
        "qhd,khd->hqk", grad_context, values, preferred_element_type=jnp.float32
    )
    grad_scores = probs * (grad_probs - jnp.sum(probs * grad_probs, axis=-1, keepdims=True))
    grad_low = grad_scores.astype(jnp.bfloat16)
    grad_query = (
        jnp.einsum("hqk,khd->qhd", grad_low, keys, preferred_element_type=jnp.float32) * scale
    )
    grad_keys = (
        jnp.einsum("hqk,qhd->khd", grad_low, query, preferred_element_type=jnp.float32) * scale
    )
    return (grad_query, grad_keys, grad_values)


def local(
    layer_input,
    segment_ids,
    qkv_weight,
    qv_bias,
    out_weight,
    up_weight,
    up_bias,
    down_weight,
    norm_gains,
    row_biases,
    cotangent,
):
    gains_all, biases_all = (
        lax.all_gather(norm_gains, ("dp", "tensor"), axis=1, tiled=True),
        lax.all_gather(row_biases, ("dp", "tensor"), axis=1, tiled=True),
    )
    shards = (qkv_weight, qv_bias, out_weight, up_weight, up_bias, down_weight)
    dp_count = lax.axis_size("dp")
    seq_len = segment_ids.shape[1]
    heads_local = qv_bias.shape[1]
    width_local = heads_local * HEAD_DIM
    scale = HEAD_DIM ** (-0.5)

    def micro_step(carry, inputs):
        rows_in, segments, grad_rows = inputs
        qkv_full, qv_full, out_full, up_full, upb_full, down_full = (
            lax.all_gather(shards[0], "dp", axis=1, tiled=True),
            lax.all_gather(shards[1], "dp", axis=2, tiled=True),
            lax.all_gather(shards[2], "dp", axis=1, tiled=True),
            lax.all_gather(shards[3], "dp", axis=0, tiled=True),
            lax.all_gather(shards[4], "dp", axis=1, tiled=True),
            lax.all_gather(shards[5], "dp", axis=1, tiled=True),
        )
        gathered = lax.all_gather(rows_in, "tensor", axis=0, tiled=True)
        projected = jnp.einsum(
            "rd,kdc->krc", gathered, qkv_full, preferred_element_type=jnp.float32
        )
        bias_flat = qv_full.reshape(2, width_local).astype(jnp.float32)
        split = (seq_len, heads_local, HEAD_DIM)
        query = (projected[0] + bias_flat[0]).astype(jnp.bfloat16).reshape(split)
        keys = projected[1].astype(jnp.bfloat16).reshape(split)
        values = (projected[2] + bias_flat[1]).astype(jnp.bfloat16).reshape(split)
        keep_mask = segments[:, None] == segments[None, :]
        attended, logsumexp = attend(query, keys, values, keep_mask, scale)
        context = attended.reshape(seq_len, width_local).astype(jnp.bfloat16)
        attention = lax.psum_scatter(
            jnp.dot(context, out_full, preferred_element_type=jnp.float32).astype(jnp.bfloat16),
            "tensor",
            scatter_dimension=0,
            tiled=True,
        ).astype(jnp.float32)
        residual_one = rows_in.astype(jnp.float32) + attention + biases_all[0]
        hidden, normed_one, inverse_one = normalize(residual_one, gains_all[0], biases_all[1])
        hidden_rows = lax.all_gather(hidden.astype(jnp.bfloat16), "tensor", axis=0, tiled=True)
        upper = jnp.dot(
            hidden_rows, up_full, preferred_element_type=jnp.float32
        ) + upb_full.reshape(-1).astype(jnp.float32)
        activated = gelu_exact(upper).astype(jnp.bfloat16)
        branch = lax.psum_scatter(
            jnp.dot(activated, down_full, preferred_element_type=jnp.float32).astype(jnp.bfloat16),
            "tensor",
            scatter_dimension=0,
            tiled=True,
        ).astype(jnp.float32)
        residual_two = hidden + branch + biases_all[2]
        result, normed_two, inverse_two = normalize(residual_two, gains_all[1], biases_all[3])
        qkv_back, qv_back, out_back, up_back, upb_back, down_back = (
            lax.all_gather(shards[0], "dp", axis=1, tiled=True),
            lax.all_gather(shards[1], "dp", axis=2, tiled=True),
            lax.all_gather(shards[2], "dp", axis=1, tiled=True),
            lax.all_gather(shards[3], "dp", axis=0, tiled=True),
            lax.all_gather(shards[4], "dp", axis=1, tiled=True),
            lax.all_gather(shards[5], "dp", axis=1, tiled=True),
        )
        grad_output = grad_rows.astype(jnp.float32)
        gain_two_grad = jnp.sum(grad_output * normed_two, axis=0)
        shift_two_grad = jnp.sum(grad_output, axis=0)
        grad_two = norm_back(grad_output, normed_two, inverse_two, gains_all[1])
        down_bias_grad = jnp.sum(grad_two, axis=0)
        branch_rows = lax.all_gather(grad_two.astype(jnp.bfloat16), "tensor", axis=0, tiled=True)
        down_grad = jnp.einsum(
            "rf,rd->fd", activated, branch_rows, preferred_element_type=jnp.float32
        )
        grad_active = jnp.einsum(
            "rd,fd->rf", branch_rows, down_back, preferred_element_type=jnp.float32
        )
        gelu_pull = jax.vjp(gelu_exact, upper)[1]
        grad_upper = gelu_pull(grad_active)[0].astype(jnp.bfloat16)
        up_bias_grad = jnp.sum(grad_upper.astype(jnp.float32), axis=0).reshape(1, -1)
        up_grad = jnp.einsum(
            "rd,rf->df", hidden_rows, grad_upper, preferred_element_type=jnp.float32
        )
        grad_hidden = grad_two + lax.psum_scatter(
            jnp.einsum("rf,df->rd", grad_upper, up_back, preferred_element_type=jnp.float32).astype(
                jnp.bfloat16
            ),
            "tensor",
            scatter_dimension=0,
            tiled=True,
        ).astype(jnp.float32)
        gain_one_grad = jnp.sum(grad_hidden * normed_one, axis=0)
        shift_one_grad = jnp.sum(grad_hidden, axis=0)
        grad_one = norm_back(grad_hidden, normed_one, inverse_one, gains_all[0])
        out_bias_grad = jnp.sum(grad_one, axis=0)
        attention_rows = lax.all_gather(grad_one.astype(jnp.bfloat16), "tensor", axis=0, tiled=True)
        out_grad = jnp.einsum(
            "rc,rd->cd", context, attention_rows, preferred_element_type=jnp.float32
        )
        grad_context = (
            jnp.einsum("rd,cd->rc", attention_rows, out_back, preferred_element_type=jnp.float32)
            .astype(jnp.bfloat16)
            .reshape(split)
        )
        grad_query, grad_keys, grad_values = attend_back(
            query, keys, values, keep_mask, logsumexp, grad_context, scale
        )
        grad_qkv = (
            jnp.stack([grad_query, grad_keys, grad_values])
            .reshape(3, seq_len, width_local)
            .astype(jnp.bfloat16)
        )
        bias_sums = jnp.sum(jnp.stack([grad_qkv[0], grad_qkv[2]]).astype(jnp.float32), axis=1)
        qv_grad = bias_sums.reshape(2, heads_local, HEAD_DIM)
        qkv_grad = jnp.einsum("rd,krc->kdc", gathered, grad_qkv, preferred_element_type=jnp.float32)
        input_grad = (
            grad_one
            + lax.psum_scatter(
                jnp.einsum(
                    "krc,kdc->rd", grad_qkv, qkv_back, preferred_element_type=jnp.float32
                ).astype(jnp.bfloat16),
                "tensor",
                scatter_dimension=0,
                tiled=True,
            ).astype(jnp.float32)
        ).astype(jnp.bfloat16)
        gains_grad = jnp.stack([gain_one_grad, gain_two_grad])
        biases_grad = jnp.stack([out_bias_grad, shift_one_grad, down_bias_grad, shift_two_grad])
        updates = (
            qkv_grad,
            qv_grad,
            out_grad,
            up_grad,
            up_bias_grad,
            down_grad,
            gains_grad,
            biases_grad,
        )
        carry = tuple((total + update for total, update in zip(carry, updates)))
        return (carry, (result.astype(jnp.bfloat16), input_grad))

    initial = (
        jnp.zeros((3, qkv_weight.shape[1] * dp_count, qkv_weight.shape[2]), jnp.float32),
        jnp.zeros((2, qv_bias.shape[1], qv_bias.shape[2] * dp_count), jnp.float32),
        jnp.zeros((out_weight.shape[0], out_weight.shape[1] * dp_count), jnp.float32),
        jnp.zeros((up_weight.shape[0] * dp_count, up_weight.shape[1]), jnp.float32),
        jnp.zeros((1, up_bias.shape[1] * dp_count), jnp.float32),
        jnp.zeros((down_weight.shape[0], down_weight.shape[1] * dp_count), jnp.float32),
        jnp.zeros(gains_all.shape, jnp.float32),
        jnp.zeros(biases_all.shape, jnp.float32),
    )
    totals, (outputs, input_grads) = lax.scan(
        micro_step, initial, (layer_input, segment_ids, cotangent)
    )
    qkv_sum, qv_sum, out_sum, up_sum, upb_sum, down_sum = (
        lax.psum_scatter(
            totals[0].astype(jnp.bfloat16), "dp", scatter_dimension=1, tiled=True
        ).astype(jnp.float32),
        lax.psum_scatter(
            totals[1].astype(jnp.bfloat16), "dp", scatter_dimension=2, tiled=True
        ).astype(jnp.float32),
        lax.psum_scatter(
            totals[2].astype(jnp.bfloat16), "dp", scatter_dimension=1, tiled=True
        ).astype(jnp.float32),
        lax.psum_scatter(
            totals[3].astype(jnp.bfloat16), "dp", scatter_dimension=0, tiled=True
        ).astype(jnp.float32),
        lax.psum_scatter(
            totals[4].astype(jnp.bfloat16), "dp", scatter_dimension=1, tiled=True
        ).astype(jnp.float32),
        lax.psum_scatter(
            totals[5].astype(jnp.bfloat16), "dp", scatter_dimension=1, tiled=True
        ).astype(jnp.float32),
    )
    gains_sum, biases_sum = (
        lax.psum_scatter(totals[6], ("dp", "tensor"), scatter_dimension=1, tiled=True),
        lax.psum_scatter(totals[7], ("dp", "tensor"), scatter_dimension=1, tiled=True),
    )
    return (
        outputs,
        input_grads,
        qkv_sum,
        qv_sum,
        out_sum,
        up_sum,
        upb_sum,
        down_sum,
        gains_sum,
        biases_sum,
    )


def solution(mesh):
    return jax.shard_map(
        local,
        mesh=mesh,
        in_specs=(
            P(None, ("dp", "tensor"), None),
            P(None, "dp"),
            P(None, "dp", "tensor"),
            P(None, "tensor", "dp"),
            P("tensor", "dp"),
            P("dp", "tensor"),
            P("tensor", "dp"),
            P("tensor", "dp"),
            P(None, ("dp", "tensor")),
            P(None, ("dp", "tensor")),
            P(None, ("dp", "tensor"), None),
        ),
        out_specs=(
            P(None, ("dp", "tensor"), None),
            P(None, ("dp", "tensor"), None),
            P(None, "dp", "tensor"),
            P(None, "tensor", "dp"),
            P("tensor", "dp"),
            P("dp", "tensor"),
            P("tensor", "dp"),
            P("tensor", "dp"),
            P(None, ("dp", "tensor")),
            P(None, ("dp", "tensor")),
        ),
        check_vma=False,
    )
```

profile of v0, /device:TPU:0, one launch (start us, length us, event | category | flops | bytes accessed | tf_op | source)
XLA Modules:
  0.0 1591.5 jit_solution(6932965279047940089)
XLA Ops:
  8.8 70.0 %all-gather.2 = f32[32,32,2]{1,2,0:T(2,128)S(1)} all-gather(f32[1,32,2]{1,2,0:T(2,128)} %bitcast.322), channel_id=1, replica_groups=mesh['dp'=16,'tensor'=2] {'dp','tensor'}, dimensions={0}, use_global_device_ids=true | all-gather | bytes 8448 | tf_op jit(solution)/shard_map/all_gather | solution.py:77
  78.8 63.9 %all-gather.1 = f32[32,32,4]{1,2,0:T(4,128)S(1)} all-gather(f32[1,32,4]{1,2,0:T(4,128)} %bitcast.321), channel_id=1, replica_groups=mesh['dp'=16,'tensor'=2] {'dp','tensor'}, dimensions={0}, use_global_device_ids=true | all-gather | bytes 16896 | tf_op jit(solution)/shard_map/all_gather | solution.py:78
  142.9 834.0 %while.29 = (s32[]{:T(128)}, f32[3,1024,512]{1,2,0:T(8,128)}, f32[2,8,64]{2,1,0:T(8,128)S(1)}, f32[512,1024]{1,0:T(8,128)}, f32[1024,2048]{1,0:T(8,128)}, /*inde...) while((s32[]{:T(128)}, f32[3,1024,512]{1,2,0:T(8,128)}, ...), condition=%wide.region_24.25_spmd.clone, body=%wide.region_0.24_spmd.clone.sunk | while | flops 21109161984 | bytes 468527744 | solution.py:224
  147.4 17.2 %all_gather.62 = bf16[2,8,64]{1,0,2:T(2,128)(2,1)S(1)} all-gather(bf16[2,8,4]{1,0,2:T(2,128)(2,1)S(1)} %get-tuple-element.616), channel_id=1, replica_groups=mesh['dp'=16,'tensor'=2] {'dp'}, dimensions={2}, use_global_device_ids=true | all-gather | bytes 2176 | tf_op jit(solution)/shard_map/while/body/eval_jaxpr/all_gather | solution.py:91
  165.5 47.4 %all-gather.17.cloned.1.call-done = bf16[3,1024,512]{2,1,0:T(8,128)(2,1)} async-done(((bf16[3,64,512]{2,1,0:T(8,128)(2,1)}), bf16[3,1024,512]{2,1,0:T(8,128)(2,1)}) %all-gather.17.cloned.1.call-update) | async-done | bytes 3145744 | tf_op jit(solution)/shard_map/while/body/eval_jaxpr/all_gather | solution.py:90
  223.9 28.0 %all-gather.19.cloned.1.call-done = bf16[512,1024]{0,1:T(8,128)(2,1)} async-done(((bf16[512,64]{0,1:T(8,128)(2,1)}), bf16[512,1024]{0,1:T(8,128)(2,1)}) %all-gather.19.cloned.1.call-update) | async-done | bytes 1048592 | tf_op jit(solution)/shard_map/while/body/eval_jaxpr/all_gather | solution.py:92
  255.6 18.7 %reduce-scatter.33.cloned.1.call-done = bf16[256,1024]{1,0:T(8,128)(2,1)} async-done(((bf16[512,1024]{1,0:T(8,128)(2,1)}), bf16[256,1024]{1,0:T(8,128)(2,1)}) %reduce-scatter.33.cloned.1.call-update) | async-done | bytes 524304 | tf_op jit(solution)/shard_map/while/body/eval_jaxpr/reduce_scatter | solution.py:109
  280.0 22.0 %all_gather.60 = bf16[1,2048]{1,0:T(2,128)(2,1)S(1)} all-gather(bf16[1,128]{1,0:T(2,128)(2,1)S(1)} %copy-done.14), channel_id=1, replica_groups=mesh['dp'=16,'tensor'=2] {'dp'}, dimensions={1}, use_global_device_ids=true | all-gather | bytes 4352 | tf_op jit(solution)/shard_map/while/body/eval_jaxpr/all_gather | solution.py:94
  301.9 25.2 %all-gather.23.cloned.1.call-done = bf16[1024,2048]{1,0:T(8,128)(2,1)} async-done(((bf16[64,2048]{1,0:T(8,128)(2,1)}), bf16[1024,2048]{1,0:T(8,128)(2,1)}) %all-gather.23.cloned.1.call-update) | async-done | bytes 4194320 | tf_op jit(solution)/shard_map/while/body/eval_jaxpr/all_gather | solution.py:93
  327.1 21.9 %all-gather.21.cloned.1.call-done = bf16[512,1024]{1,0:T(8,128)(2,1)} async-done(((bf16[256,1024]{1,0:T(8,128)(2,1)}), bf16[512,1024]{1,0:T(8,128)(2,1)}) %all-gather.21.cloned.1.call-update) | async-done | bytes 1048592 | tf_op jit(solution)/shard_map/while/body/eval_jaxpr/all_gather | solution.py:117
  349.0 15.2 multiply_convert_fusion.4
  364.2 37.9 %all-gather.25.cloned.1.call-done = bf16[2048,1024]{0,1:T(8,128)(2,1)} async-done(((bf16[2048,64]{0,1:T(8,128)(2,1)}), bf16[2048,1024]{0,1:T(8,128)(2,1)}) %all-gather.25.cloned.1.call-update) | async-done | bytes 4194320 | tf_op jit(solution)/shard_map/while/body/eval_jaxpr/all_gather | solution.py:95
  402.1 6.3 convolution_convert_fusion.9
  408.5 18.9 %reduce-scatter.35.cloned.1.call-done = bf16[256,1024]{1,0:T(8,128)(2,1)} async-done(((bf16[512,1024]{1,0:T(8,128)(2,1)}), bf16[256,1024]{1,0:T(8,128)(2,1)}) %reduce-scatter.35.cloned.1.call-update) | async-done | bytes 524304 | tf_op jit(solution)/shard_map/while/body/eval_jaxpr/reduce_scatter | solution.py:122
  433.6 21.3 %all-gather.27.cloned.1.call-done = bf16[512,1024]{1,0:T(8,128)(2,1)} async-done(((bf16[256,1024]{1,0:T(8,128)(2,1)}), bf16[512,1024]{1,0:T(8,128)(2,1)}) %all-gather.27.cloned.1.call-update) | async-done | bytes 1048592 | tf_op jit(solution)/shard_map/while/body/eval_jaxpr/all_gather | solution.py:143
  454.9 8.7 convert_reduce_fusion.6
  470.7 18.2 %reduce-scatter.37.cloned.1.call-done = bf16[256,1024]{1,0:T(8,128)(2,1)} async-done(((bf16[512,1024]{1,0:T(8,128)(2,1)}), bf16[256,1024]{1,0:T(8,128)(2,1)}) %reduce-scatter.37.cloned.1.call-update) | async-done | bytes 524304 | tf_op jit(solution)/shard_map/while/body/eval_jaxpr/reduce_scatter | solution.py:156
  494.0 7.7 select_add_fusion.11
  501.8 5.7 select_add_fusion.10
  507.4 7.8 all-gather.29.cloned.1.call-done
  543.2 12.2 reduce-scatter.39.cloned.1.call-done
  561.7 21.4 %all_gather.62 = bf16[2,8,64]{1,0,2:T(2,128)(2,1)S(1)} all-gather(bf16[2,8,4]{1,0,2:T(2,128)(2,1)S(1)} %get-tuple-element.616), channel_id=1, replica_groups=mesh['dp'=16,'tensor'=2] {'dp'}, dimensions={2}, use_global_device_ids=true | all-gather | bytes 2176 | tf_op jit(solution)/shard_map/while/body/eval_jaxpr/all_gather | solution.py:91
  583.5 45.9 %all-gather.17.cloned.1.call-done = bf16[3,1024,512]{2,1,0:T(8,128)(2,1)} async-done(((bf16[3,64,512]{2,1,0:T(8,128)(2,1)}), bf16[3,1024,512]{2,1,0:T(8,128)(2,1)}) %all-gather.17.cloned.1.call-update) | async-done | bytes 3145744 | tf_op jit(solution)/shard_map/while/body/eval_jaxpr/all_gather | solution.py:90
  640.4 27.8 %all-gather.19.cloned.1.call-done = bf16[512,1024]{0,1:T(8,128)(2,1)} async-done(((bf16[512,64]{0,1:T(8,128)(2,1)}), bf16[512,1024]{0,1:T(8,128)(2,1)}) %all-gather.19.cloned.1.call-update) | async-done | bytes 1048592 | tf_op jit(solution)/shard_map/while/body/eval_jaxpr/all_gather | solution.py:92
  671.9 18.7 %reduce-scatter.33.cloned.1.call-done = bf16[256,1024]{1,0:T(8,128)(2,1)} async-done(((bf16[512,1024]{1,0:T(8,128)(2,1)}), bf16[256,1024]{1,0:T(8,128)(2,1)}) %reduce-scatter.33.cloned.1.call-update) | async-done | bytes 524304 | tf_op jit(solution)/shard_map/while/body/eval_jaxpr/reduce_scatter | solution.py:109
  696.3 21.5 %all_gather.60 = bf16[1,2048]{1,0:T(2,128)(2,1)S(1)} all-gather(bf16[1,128]{1,0:T(2,128)(2,1)S(1)} %copy-done.14), channel_id=1, replica_groups=mesh['dp'=16,'tensor'=2] {'dp'}, dimensions={1}, use_global_device_ids=true | all-gather | bytes 4352 | tf_op jit(solution)/shard_map/while/body/eval_jaxpr/all_gather | solution.py:94
  717.8 25.7 %all-gather.23.cloned.1.call-done = bf16[1024,2048]{1,0:T(8,128)(2,1)} async-done(((bf16[64,2048]{1,0:T(8,128)(2,1)}), bf16[1024,2048]{1,0:T(8,128)(2,1)}) %all-gather.23.cloned.1.call-update) | async-done | bytes 4194320 | tf_op jit(solution)/shard_map/while/body/eval_jaxpr/all_gather | solution.py:93
  743.5 21.9 %all-gather.21.cloned.1.call-done = bf16[512,1024]{1,0:T(8,128)(2,1)} async-done(((bf16[256,1024]{1,0:T(8,128)(2,1)}), bf16[512,1024]{1,0:T(8,128)(2,1)}) %all-gather.21.cloned.1.call-update) | async-done | bytes 1048592 | tf_op jit(solution)/shard_map/while/body/eval_jaxpr/all_gather | solution.py:117
  765.3 15.2 multiply_convert_fusion.4
  780.6 37.9 %all-gather.25.cloned.1.call-done = bf16[2048,1024]{0,1:T(8,128)(2,1)} async-done(((bf16[2048,64]{0,1:T(8,128)(2,1)}), bf16[2048,1024]{0,1:T(8,128)(2,1)}) %all-gather.25.cloned.1.call-update) | async-done | bytes 4194320 | tf_op jit(solution)/shard_map/while/body/eval_jaxpr/all_gather | solution.py:95
  818.5 6.2 convolution_convert_fusion.9
  824.8 18.9 %reduce-scatter.35.cloned.1.call-done = bf16[256,1024]{1,0:T(8,128)(2,1)} async-done(((bf16[512,1024]{1,0:T(8,128)(2,1)}), bf16[256,1024]{1,0:T(8,128)(2,1)}) %reduce-scatter.35.cloned.1.call-update) | async-done | bytes 524304 | tf_op jit(solution)/shard_map/while/body/eval_jaxpr/reduce_scatter | solution.py:122
  850.0 21.2 %all-gather.27.cloned.1.call-done = bf16[512,1024]{1,0:T(8,128)(2,1)} async-done(((bf16[256,1024]{1,0:T(8,128)(2,1)}), bf16[512,1024]{1,0:T(8,128)(2,1)}) %all-gather.27.cloned.1.call-update) | async-done | bytes 1048592 | tf_op jit(solution)/shard_map/while/body/eval_jaxpr/all_gather | solution.py:143
  871.2 8.7 convert_reduce_fusion.6
  887.0 18.2 %reduce-scatter.37.cloned.1.call-done = bf16[256,1024]{1,0:T(8,128)(2,1)} async-done(((bf16[512,1024]{1,0:T(8,128)(2,1)}), bf16[256,1024]{1,0:T(8,128)(2,1)}) %reduce-scatter.37.cloned.1.call-update) | async-done | bytes 524304 | tf_op jit(solution)/shard_map/while/body/eval_jaxpr/reduce_scatter | solution.py:156
  910.4 10.1 select_add_fusion.11
  920.5 9.1 select_add_fusion.10
  956.1 7.7 bitcast_add_fusion.2
  963.7 8.3 reduce-scatter.39.cloned.1.call-done
  987.3 6.0 convert_element_type.143
  993.4 7.4 copy.56
  1002.7 61.3 %all-reduce = bf16[2,8,64]{1,2,0:T(8,128)(2,1)S(1)} all-reduce(bf16[2,8,64]{1,2,0:T(8,128)(2,1)S(1)} %copy.54), channel_id=8, replica_groups=mesh['dp'=16,'tensor'=2] {'dp'}, use_global_device_ids=true, to_apply=%region_26.27.clone | all-reduce | flops 1024 | bytes 4096
  1066.0 107.1 %reduce-scatter.29.cloned.1.call-done = f32[32,2]{1,0:T(8,128)} async-done(((f32[1024,2]{1,0:T(8,128)}), f32[32,2]{1,0:T(8,128)}) %reduce-scatter.29.cloned.1.call-update) | async-done | bytes 272
  1174.5 130.3 %reduce-scatter.31.cloned.1.call-done = f32[32,4]{1,0:T(8,128)} async-done(((f32[1024,4]{1,0:T(8,128)}), f32[32,4]{1,0:T(8,128)}) %reduce-scatter.31.cloned.1.call-update) | async-done | bytes 528
  1306.1 56.1 %reduce-scatter.21.cloned.1.call-done = bf16[512,64]{0,1:T(8,128)(2,1)} async-done(((bf16[512,1024]{0,1:T(8,128)(2,1)}), bf16[512,64]{0,1:T(8,128)(2,1)}) %reduce-scatter.21.cloned.1.call-update) | async-done | bytes 65552 | tf_op jit(solution)/shard_map/reduce_scatter | solution.py:234
  1363.7 67.5 %reduce-scatter.19.cloned.1.call-done = bf16[3,64,512]{2,1,0:T(8,128)(2,1)} async-done(((bf16[3,1024,512]{2,1,0:T(8,128)(2,1)}), bf16[3,64,512]{2,1,0:T(8,128)(2,1)}) %reduce-scatter.19.cloned.1.call-update) | async-done | bytes 196624 | tf_op jit(solution)/shard_map/reduce_scatter | solution.py:228
  1433.0 73.4 %reduce-scatter.23.cloned.1.call-done = bf16[64,2048]{1,0:T(8,128)(2,1)} async-done(((bf16[1024,2048]{1,0:T(8,128)(2,1)}), bf16[64,2048]{1,0:T(8,128)(2,1)}) %reduce-scatter.23.cloned.1.call-update) | async-done | bytes 262160 | tf_op jit(solution)/shard_map/reduce_scatter | solution.py:237
  1508.1 73.9 %reduce-scatter.25.cloned.1.call-done = bf16[2048,64]{0,1:T(8,128)(2,1)} async-done(((bf16[2048,1024]{0,1:T(8,128)(2,1)}), bf16[2048,64]{0,1:T(8,128)(2,1)}) %reduce-scatter.25.cloned.1.call-update) | async-done | bytes 262160 | tf_op jit(solution)/shard_map/reduce_scatter | solution.py:243
  (286 shorter events, 168.5 us)
Async XLA Ops:
  143.2 22.3 %all-gather.15.cloned.1.call-start = ((), (), s32[]{:S(2)}) async-start(), calls=%async_computation.18 | async-start | bytes 1572864 | tf_op jit(solution)/shard_map/while/body/eval_jaxpr/all_gather | solution.py:97
  145.2 67.8 %all-gather.17.cloned.1.call-start = ((), (), s32[]{:S(2)}) async-start(), calls=%async_computation.19 | async-start | bytes 3342336 | tf_op jit(solution)/shard_map/while/body/eval_jaxpr/all_gather | solution.py:90
  145.9 106.0 %all-gather.19.cloned.1.call-start = ((), (), s32[]{:S(2)}) async-start(), calls=%async_computation.20 | async-start | bytes 1114112 | tf_op jit(solution)/shard_map/while/body/eval_jaxpr/all_gather | solution.py:92
  146.6 127.6 %reduce-scatter.33.cloned.1.call-start = ((), (), s32[]{:S(2)}) async-start(), calls=%async_computation.21 | async-start | bytes 1572864 | tf_op jit(solution)/shard_map/while/body/eval_jaxpr/reduce_scatter | solution.py:109
  223.9 55.3 %copy-start.12 = (bf16[8,64,512]{2,1,0:T(8,128)(2,1)}, bf16[8,64,512]{2,1,0:T(8,128)(2,1)S(1)}, u32[]{:S(2)}) copy-start(bf16[8,64,512]{2,1,0:T(8,128)(2,1)S(1)} %fusion.158) | copy-start | bytes 1572868 | tf_op jit(solution)/shard_map/while
  223.9 50.4 %copy-start.2 = (bf16[2,256,1024]{2,1,0:T(8,128)(2,1)S(1)}, bf16[2,256,1024]{2,1,0:T(8,128)(2,1)}, u32[]{:S(2)}) copy-start(bf16[2,256,1024]{2,1,0:T(8,128)(2,1)} %get-tuple-element.613) | copy-start | bytes 3145732 | tf_op jit(solution)/shard_map/while
  251.9 28.1 %copy-start.14 = (bf16[1,128]{1,0:T(2,128)(2,1)S(1)}, bf16[1,128]{1,0:T(2,128)(2,1)}, u32[]{:S(2)}) copy-start(bf16[1,128]{1,0:T(2,128)(2,1)} %get-tuple-element.621) | copy-start | bytes 772 | tf_op jit(solution)/shard_map/while
  254.9 72.2 %all-gather.23.cloned.1.call-start = ((), (), s32[]{:S(2)}) async-start(), calls=%async_computation.23 | async-start | bytes 4456448 | tf_op jit(solution)/shard_map/while/body/eval_jaxpr/all_gather | solution.py:93
  255.5 93.5 %all-gather.21.cloned.1.call-start = ((), (), s32[]{:S(2)}) async-start(), calls=%async_computation.22 | async-start | bytes 1572864 | tf_op jit(solution)/shard_map/while/body/eval_jaxpr/all_gather | solution.py:117
  279.1 123.0 %all-gather.25.cloned.1.call-start = ((), (), s32[]{:S(2)}) async-start(), calls=%async_computation.24 | async-start | bytes 4456448 | tf_op jit(solution)/shard_map/while/body/eval_jaxpr/all_gather | solution.py:95
  279.9 147.5 %reduce-scatter.35.cloned.1.call-start = ((), (), s32[]{:S(2)}) async-start(), calls=%async_computation.25 | async-start | bytes 1572864 | tf_op jit(solution)/shard_map/while/body/eval_jaxpr/reduce_scatter | solution.py:122
  402.1 25.2 %copy-start.1 = (bf16[256,1024]{1,0:T(8,128)(2,1)S(1)}, bf16[256,1024]{1,0:T(8,128)(2,1)}, u32[]{:S(2)}) copy-start(bf16[256,1024]{1,0:T(8,128)(2,1)} %reduce-scatter.33.cloned.1.call-done) | copy-start | bytes 1572868 | tf_op jit(solution)/shard_map/while
  408.4 46.5 %all-gather.27.cloned.1.call-start = ((), (), s32[]{:S(2)}) async-start(), calls=%async_computation.26 | async-start | bytes 1572864 | tf_op jit(solution)/shard_map/while/body/eval_jaxpr/all_gather | solution.py:143
  433.4 55.5 %reduce-scatter.37.cloned.1.call-start = ((), (), s32[]{:S(2)}) async-start(), calls=%async_computation.27 | async-start | bytes 1572864 | tf_op jit(solution)/shard_map/while/body/eval_jaxpr/reduce_scatter | solution.py:156
  454.9 10.1 copy-start.15
  468.4 46.8 %all-gather.29.cloned.1.call-start = ((), (), s32[]{:S(2)}) async-start(), calls=%async_computation.28 | async-start | bytes 1572864 | tf_op jit(solution)/shard_map/while/body/eval_jaxpr/all_gather | solution.py:168
  493.8 61.6 %reduce-scatter.39.cloned.1.call-start = ((), (), s32[]{:S(2)}) async-start(), calls=%async_computation.29 | async-start | bytes 1572864 | tf_op jit(solution)/shard_map/while/body/eval_jaxpr/reduce_scatter | solution.py:190
  494.0 7.7 copy-start.8
  501.7 13.5 copy-start.17
  517.2 9.9 slice-start
  557.8 25.7 %all-gather.15.cloned.1.call-start = ((), (), s32[]{:S(2)}) async-start(), calls=%async_computation.18 | async-start | bytes 1572864 | tf_op jit(solution)/shard_map/while/body/eval_jaxpr/all_gather | solution.py:97
  559.8 69.6 %all-gather.17.cloned.1.call-start = ((), (), s32[]{:S(2)}) async-start(), calls=%async_computation.19 | async-start | bytes 3342336 | tf_op jit(solution)/shard_map/while/body/eval_jaxpr/all_gather | solution.py:90
  560.4 107.9 %all-gather.19.cloned.1.call-start = ((), (), s32[]{:S(2)}) async-start(), calls=%async_computation.20 | async-start | bytes 1114112 | tf_op jit(solution)/shard_map/while/body/eval_jaxpr/all_gather | solution.py:92
  561.0 129.7 %reduce-scatter.33.cloned.1.call-start = ((), (), s32[]{:S(2)}) async-start(), calls=%async_computation.21 | async-start | bytes 1572864 | tf_op jit(solution)/shard_map/while/body/eval_jaxpr/reduce_scatter | solution.py:109
  640.4 55.1 %copy-start.12 = (bf16[8,64,512]{2,1,0:T(8,128)(2,1)}, bf16[8,64,512]{2,1,0:T(8,128)(2,1)S(1)}, u32[]{:S(2)}) copy-start(bf16[8,64,512]{2,1,0:T(8,128)(2,1)S(1)} %fusion.158) | copy-start | bytes 1572868 | tf_op jit(solution)/shard_map/while
  640.4 50.2 %copy-start.2 = (bf16[2,256,1024]{2,1,0:T(8,128)(2,1)S(1)}, bf16[2,256,1024]{2,1,0:T(8,128)(2,1)}, u32[]{:S(2)}) copy-start(bf16[2,256,1024]{2,1,0:T(8,128)(2,1)} %get-tuple-element.613) | copy-start | bytes 3145732 | tf_op jit(solution)/shard_map/while
  668.2 28.1 %copy-start.14 = (bf16[1,128]{1,0:T(2,128)(2,1)S(1)}, bf16[1,128]{1,0:T(2,128)(2,1)}, u32[]{:S(2)}) copy-start(bf16[1,128]{1,0:T(2,128)(2,1)} %get-tuple-element.621) | copy-start | bytes 772 | tf_op jit(solution)/shard_map/while
  671.2 72.2 %all-gather.23.cloned.1.call-start = ((), (), s32[]{:S(2)}) async-start(), calls=%async_computation.23 | async-start | bytes 4456448 | tf_op jit(solution)/shard_map/while/body/eval_jaxpr/all_gather | solution.py:93
  671.8 93.5 %all-gather.21.cloned.1.call-start = ((), (), s32[]{:S(2)}) async-start(), calls=%async_computation.22 | async-start | bytes 1572864 | tf_op jit(solution)/shard_map/while/body/eval_jaxpr/all_gather | solution.py:117
  695.5 123.0 %all-gather.25.cloned.1.call-start = ((), (), s32[]{:S(2)}) async-start(), calls=%async_computation.24 | async-start | bytes 4456448 | tf_op jit(solution)/shard_map/while/body/eval_jaxpr/all_gather | solution.py:95
  696.3 147.5 %reduce-scatter.35.cloned.1.call-start = ((), (), s32[]{:S(2)}) async-start(), calls=%async_computation.25 | async-start | bytes 1572864 | tf_op jit(solution)/shard_map/while/body/eval_jaxpr/reduce_scatter | solution.py:122
  818.5 25.2 %copy-start.1 = (bf16[256,1024]{1,0:T(8,128)(2,1)S(1)}, bf16[256,1024]{1,0:T(8,128)(2,1)}, u32[]{:S(2)}) copy-start(bf16[256,1024]{1,0:T(8,128)(2,1)} %reduce-scatter.33.cloned.1.call-done) | copy-start | bytes 1572868 | tf_op jit(solution)/shard_map/while
  824.8 46.5 %all-gather.27.cloned.1.call-start = ((), (), s32[]{:S(2)}) async-start(), calls=%async_computation.26 | async-start | bytes 1572864 | tf_op jit(solution)/shard_map/while/body/eval_jaxpr/all_gather | solution.py:143
  849.7 55.5 %reduce-scatter.37.cloned.1.call-start = ((), (), s32[]{:S(2)}) async-start(), calls=%async_computation.27 | async-start | bytes 1572864 | tf_op jit(solution)/shard_map/while/body/eval_jaxpr/reduce_scatter | solution.py:156
  871.2 10.1 copy-start.15
  884.7 46.8 %all-gather.29.cloned.1.call-start = ((), (), s32[]{:S(2)}) async-start(), calls=%async_computation.28 | async-start | bytes 1572864 | tf_op jit(solution)/shard_map/while/body/eval_jaxpr/all_gather | solution.py:168
  910.1 61.9 %reduce-scatter.39.cloned.1.call-start = ((), (), s32[]{:S(2)}) async-start(), calls=%async_computation.29 | async-start | bytes 1572864 | tf_op jit(solution)/shard_map/while/body/eval_jaxpr/reduce_scatter | solution.py:190
  910.4 10.1 copy-start.8
  910.4 10.1 copy-start.10
  920.5 11.0 copy-start.17
  933.6 10.2 slice-start
  976.9 87.7 %reduce-scatter.27.cloned.1.call-start = ((), (), s32[]{:S(2)}) async-start(), calls=%async_computation.15 | async-start | bytes 557056
  978.0 195.1 %reduce-scatter.29.cloned.1.call-start = ((), (), s32[]{:S(2)}) async-start(), calls=%async_computation.16 | async-start | bytes 540672
  979.2 325.6 %reduce-scatter.31.cloned.1.call-start = ((), (), s32[]{:S(2)}) async-start(), calls=%async_computation.17 | async-start | bytes 540672
  980.3 381.9 %reduce-scatter.21.cloned.1.call-start = ((), (), s32[]{:S(2)}) async-start(), calls=%async_computation.12 | async-start | bytes 1114112 | tf_op jit(solution)/shard_map/reduce_scatter | solution.py:234
  981.8 449.5 %reduce-scatter.19.cloned.1.call-start = ((), (), s32[]{:S(2)}) async-start(), calls=%async_computation.11 | async-start | bytes 3342336 | tf_op jit(solution)/shard_map/reduce_scatter | solution.py:228
  987.3 519.1 %reduce-scatter.23.cloned.1.call-start = ((), (), s32[]{:S(2)}) async-start(), calls=%async_computation.13 | async-start | bytes 4456448 | tf_op jit(solution)/shard_map/reduce_scatter | solution.py:237
  993.4 588.7 %reduce-scatter.25.cloned.1.call-start = ((), (), s32[]{:S(2)}) async-start(), calls=%async_computation.14 | async-start | bytes 4456448 | tf_op jit(solution)/shard_map/reduce_scatter | solution.py:243
  (23 other events, 73.9 us)
Sparse Core Ops, SparseCore 0:
  146.2 19.2 all-gather.14
  167.7 45.1 all-gather.16
  215.1 36.7 all-gather.18
  255.0 19.2 reduce-scatter.32
  276.5 50.5 all-gather.22
  329.2 19.7 all-gather.20
  351.4 50.7 all-gather.24
  408.5 18.7 reduce-scatter.34
  433.5 21.3 all-gather.26
  468.5 20.3 reduce-scatter.36
  493.9 21.2 all-gather.28
  535.1 20.3 reduce-scatter.38
  560.8 21.2 all-gather.14
  584.2 45.1 all-gather.16
  631.4 36.7 all-gather.18
  671.4 19.2 reduce-scatter.32
  692.9 50.5 all-gather.22
  745.5 19.7 all-gather.20
  767.7 50.7 all-gather.24
  824.9 18.7 reduce-scatter.34
  849.9 21.3 all-gather.26
  884.9 20.3 reduce-scatter.36
  910.2 21.2 all-gather.28
  951.7 20.3 reduce-scatter.38
Sparse Core Ops, SparseCore 1:
  981.5 55.8 reduce-scatter.26
  1040.1 132.9 reduce-scatter.28
  1175.2 129.5 reduce-scatter.30
  1308.8 53.4 reduce-scatter.20
  1366.0 65.1 reduce-scatter.18
  1435.1 71.1 reduce-scatter.22
  1510.5 71.4 reduce-scatter.24
where the time goes:
time: 1590 us
  waiting for transfers between devices  1020 us (64%)
  blocking collectives  277 us (17%)
  matrix products  174 us (11%)
  other arithmetic  62.4 us (4%)
  local copies, waits for them, and re-layouts  35.9 us (2%)
  between operations  16.6 us (1%)
    unnamed x10, waiting for transfers between devices  238 us
    all_gather x2, waiting for transfers between devices, micro_step(): lax.all_gather(shards[0], 'dp', axis=1, tiled=True)  93.3 us
    all_gather x2, waiting for transfers between devices, micro_step(): lax.all_gather(shards[5], 'dp', axis=1, tiled=True)  75.8 us
    reduce_scatter x1, waiting for transfers between devices, local(): lax.psum_scatter(totals[5].astype(jnp.bfloat16), 'dp', scatter_dimension=...  73.9 us
    reduce_scatter x1, waiting for transfers between devices, local(): lax.psum_scatter(totals[3].astype(jnp.bfloat16), 'dp', scatter_dimension=...  73.4 us
    all_gather x1, blocking collectives, local(): lax.all_gather(norm_gains, ('dp', 'tensor'), axis=1, tiled=True)  70 us
    reduce_scatter x1, waiting for transfers between devices, local(): lax.psum_scatter(totals[0].astype(jnp.bfloat16), 'dp', scatter_dimension=...  67.5 us
    all_gather x1, blocking collectives, local(): lax.all_gather(row_biases, ('dp', 'tensor'), axis=1, tiled=True)  63.9 us
  transfers between devices with their start and end apart: 31, of which 29 were waited for; matrix products, arithmetic and copies ran while one was open for 9% of the time, Pallas kernels for 0%

commit v1 on v0

--- a/solution.py
+++ b/solution.py
@@ -4,6 +4,25 @@
 from jax.sharding import PartitionSpec as P
 
 HEAD_DIM = 64
+
+
+def _serve_plane(inp, axis_id="dp"):
+    size_here = lax.axis_size(axis_id)
+    shelf = []
+    for ii in range(size_here):
+        shelf.append((ii, (ii + 1) % size_here))
+    log = []
+    for ii in range(size_here):
+        log.append((ii, (ii - 1) % size_here))
+    part_now, state_now = ([inp], [inp])
+    for _ in range(size_here // 2):
+        main = lax.ppermute(part_now[-1], axis_id, shelf)
+        part_now.append(main)
+    for _ in range((size_here - 1) // 2):
+        a_now = lax.ppermute(state_now[-1], axis_id, perm=log)
+        state_now.append(a_now)
+    answer = jnp.concatenate([*part_now[::-1], *state_now[1:]], 1)
+    return jnp.roll(answer, (lax.axis_index(axis_id) - size_here // 2) * inp.shape[1], 1)
 
 
 def gelu_exact(values):
@@ -89,7 +108,7 @@
         qkv_full, qv_full, out_full, up_full, upb_full, down_full = (
             lax.all_gather(shards[0], "dp", axis=1, tiled=True),
             lax.all_gather(shards[1], "dp", axis=2, tiled=True),
-            lax.all_gather(shards[2], "dp", axis=1, tiled=True),
+            _serve_plane(shards[2]),
             lax.all_gather(shards[3], "dp", axis=0, tiled=True),
             lax.all_gather(shards[4], "dp", axis=1, tiled=True),
             lax.all_gather(shards[5], "dp", axis=1, tiled=True),

time: 1590 us -> 1670 us (1.050)
  starting transfers between devices: 2.18 us -> 34.5 us
  waiting for transfers between devices: 1020 us -> 1050 us
    all_gather x2, waiting for transfers between devices: 9.74 us -> 44.9 us  [micro_step(): lax.all_gather(grad_one.astype(jnp.bfloat16), 'tensor', axis=0, tiled=True)]
    ppermute x0 -> x15, starting transfers between devices: none -> 32.3 us  [the longest x7 31.8 us: _serve_plane(): a_now = lax.ppermute(state_now[-1], axis_id, perm=log)]
    ppermute x0 -> x15, waiting for transfers between devices: none -> 18.9 us  [the longest x8 18.9 us: _serve_plane(): main = lax.ppermute(part_now[-1], axis_id, shelf)]
    all_gather x2, waiting for transfers between devices: 55.8 us -> 37.6 us  [micro_step(): lax.all_gather(shards[2], 'dp', axis=1, tiled=True)]
  transfers between devices with their start and end apart: 31 -> 46, of which waited for: 29 -> 37; matrix products, arithmetic and copies ran while one was open for 9% -> 9% of each run, Pallas kernels for 0% -> 0%
where the time goes in v1:
time: 1670 us
  waiting for transfers between devices  1050 us (63%)
  blocking collectives  277 us (17%)
  matrix products  173 us (10%)
  other arithmetic  64.5 us (4%)
  local copies, waits for them, and re-layouts  43.8 us (3%)
  starting transfers between devices  34.5 us (2%)
    unnamed x10, waiting for transfers between devices  237 us
    all_gather x2, waiting for transfers between devices, micro_step(): lax.all_gather(shards[0], 'dp', axis=1, tiled=True)  94.7 us
    all_gather x2, waiting for transfers between devices, micro_step(): lax.all_gather(shards[5], 'dp', axis=1, tiled=True)  75.4 us
    reduce_scatter x1, waiting for transfers between devices, local(): lax.psum_scatter(totals[5].astype(jnp.bfloat16), 'dp', scatter_dimension=...  73.8 us
    reduce_scatter x1, waiting for transfers between devices, local(): lax.psum_scatter(totals[3].astype(jnp.bfloat16), 'dp', scatter_dimension=...  73.3 us
    all_gather x1, blocking collectives, local(): lax.all_gather(norm_gains, ('dp', 'tensor'), axis=1, tiled=True)  69.4 us
    reduce_scatter x1, waiting for transfers between devices, local(): lax.psum_scatter(totals[0].astype(jnp.bfloat16), 'dp', scatter_dimension=...  67.5 us
    all_gather x1, blocking collectives, local(): lax.all_gather(row_biases, ('dp', 'tensor'), axis=1, tiled=True)  63.9 us
  transfers between devices with their start and end apart: 46, of which 37 were waited for; matrix products, arithmetic and copies ran while one was open for 9% of the time, Pallas kernels for 0%

profile of v1, /device:TPU:0, one launch (start us, length us, event | category | flops | bytes accessed | tf_op | source)
XLA Modules:
  0.0 1667.8 jit_solution(15551771960357355896)
XLA Ops:
  61.0 69.4 %all-gather.2 = f32[32,32,2]{1,2,0:T(2,128)S(1)} all-gather(f32[1,32,2]{1,2,0:T(2,128)} %bitcast.319), channel_id=1, replica_groups=mesh['dp'=16,'tensor'=2] {'dp','tensor'}, dimensions={0}, use_global_device_ids=true | all-gather | bytes 8448 | tf_op jit(solution)/shard_map/all_gather | solution.py:96
  130.6 63.9 %all-gather.1 = f32[32,32,4]{1,2,0:T(4,128)S(1)} all-gather(f32[1,32,4]{1,2,0:T(4,128)} %bitcast.318), channel_id=1, replica_groups=mesh['dp'=16,'tensor'=2] {'dp','tensor'}, dimensions={0}, use_global_device_ids=true | all-gather | bytes 16896 | tf_op jit(solution)/shard_map/all_gather | solution.py:97
  194.6 8.5 concatenate.13
  203.2 850.5 %while.31 = (s32[]{:T(128)}, f32[3,1024,512]{1,2,0:T(8,128)}, f32[2,8,64]{2,1,0:T(8,128)S(1)}, f32[512,1024]{1,0:T(8,128)}, f32[1024,2048]{1,0:T(8,128)}, /*inde...) while((s32[]{:T(128)}, f32[3,1024,512]{1,2,0:T(8,128)}, ...), condition=%wide.region_24.25_spmd.clone, body=%wide.region_0.24_spmd.clone.sunk | while | flops 21109161984 | bytes 474818496 | solution.py:243
  205.4 17.2 %all_gather.91 = bf16[2,8,64]{1,0,2:T(2,128)(2,1)S(1)} all-gather(bf16[2,8,4]{1,0,2:T(2,128)(2,1)S(1)} %get-tuple-element.827), channel_id=1, replica_groups=mesh['dp'=16,'tensor'=2] {'dp'}, dimensions={2}, use_global_device_ids=true | all-gather | bytes 2176 | tf_op jit(solution)/shard_map/while/body/eval_jaxpr/all_gather | solution.py:110
  225.9 47.4 %all-gather.17.cloned.1.call-done = bf16[3,1024,512]{2,1,0:T(8,128)(2,1)} async-done(((bf16[3,64,512]{2,1,0:T(8,128)(2,1)}), bf16[3,1024,512]{2,1,0:T(8,128)(2,1)}) %all-gather.17.cloned.1.call-update) | async-done | bytes 3145744 | tf_op jit(solution)/shard_map/while/body/eval_jaxpr/all_gather | solution.py:109
  286.9 18.6 %reduce-scatter.33.cloned.1.call-done = bf16[256,1024]{1,0:T(8,128)(2,1)} async-done(((bf16[512,1024]{1,0:T(8,128)(2,1)}), bf16[256,1024]{1,0:T(8,128)(2,1)}) %reduce-scatter.33.cloned.1.call-update) | async-done | bytes 524304 | tf_op jit(solution)/shard_map/while/body/eval_jaxpr/reduce_scatter | solution.py:128
  311.0 21.7 %all_gather.89 = bf16[1,2048]{1,0:T(2,128)(2,1)S(1)} all-gather(bf16[1,128]{1,0:T(2,128)(2,1)S(1)} %get-tuple-element.832), channel_id=1, replica_groups=mesh['dp'=16,'tensor'=2] {'dp'}, dimensions={1}, use_global_device_ids=true | all-gather | bytes 4352 | tf_op jit(solution)/shard_map/while/body/eval_jaxpr/all_gather | solution.py:113
  332.8 25.6 %all-gather.21.cloned.1.call-done = bf16[1024,2048]{1,0:T(8,128)(2,1)} async-done(((bf16[64,2048]{1,0:T(8,128)(2,1)}), bf16[1024,2048]{1,0:T(8,128)(2,1)}) %all-gather.21.cloned.1.call-update) | async-done | bytes 4194320 | tf_op jit(solution)/shard_map/while/body/eval_jaxpr/all_gather | solution.py:112
  358.4 21.9 %all-gather.19.cloned.1.call-done = bf16[512,1024]{1,0:T(8,128)(2,1)} async-done(((bf16[256,1024]{1,0:T(8,128)(2,1)}), bf16[512,1024]{1,0:T(8,128)(2,1)}) %all-gather.19.cloned.1.call-update) | async-done | bytes 1048592 | tf_op jit(solution)/shard_map/while/body/eval_jaxpr/all_gather | solution.py:136
  380.3 15.2 multiply_convert_fusion.4
  395.5 37.6 %all-gather.23.cloned.1.call-done = bf16[2048,1024]{0,1:T(8,128)(2,1)} async-done(((bf16[2048,64]{0,1:T(8,128)(2,1)}), bf16[2048,1024]{0,1:T(8,128)(2,1)}) %all-gather.23.cloned.1.call-update) | async-done | bytes 4194320 | tf_op jit(solution)/shard_map/while/body/eval_jaxpr/all_gather | solution.py:114
  433.1 6.2 convolution_convert_fusion.9
  439.4 18.9 %reduce-scatter.35.cloned.1.call-done = bf16[256,1024]{1,0:T(8,128)(2,1)} async-done(((bf16[512,1024]{1,0:T(8,128)(2,1)}), bf16[256,1024]{1,0:T(8,128)(2,1)}) %reduce-scatter.35.cloned.1.call-update) | async-done | bytes 524304 | tf_op jit(solution)/shard_map/while/body/eval_jaxpr/reduce_scatter | solution.py:141
  464.5 21.3 %all-gather.25.cloned.1.call-done = bf16[512,1024]{1,0:T(8,128)(2,1)} async-done(((bf16[256,1024]{1,0:T(8,128)(2,1)}), bf16[512,1024]{1,0:T(8,128)(2,1)}) %all-gather.25.cloned.1.call-update) | async-done | bytes 1048592 | tf_op jit(solution)/shard_map/while/body/eval_jaxpr/all_gather | solution.py:162
  485.8 8.7 convert_reduce_fusion.6
  502.2 17.6 %reduce-scatter.37.cloned.1.call-done = bf16[256,1024]{1,0:T(8,128)(2,1)} async-done(((bf16[512,1024]{1,0:T(8,128)(2,1)}), bf16[256,1024]{1,0:T(8,128)(2,1)}) %reduce-scatter.37.cloned.1.call-update) | async-done | bytes 524304 | tf_op jit(solution)/shard_map/while/body/eval_jaxpr/reduce_scatter | solution.py:175
  525.0 7.7 select_add_fusion.11
  538.3 21.7 %all-gather.29.cloned.1.call-done = bf16[512,1024]{0,1:T(8,128)(2,1)} async-done(((bf16[512,64]{0,1:T(8,128)(2,1)}), bf16[512,1024]{0,1:T(8,128)(2,1)}) %all-gather.29.cloned.1.call-update) | async-done | bytes 1048592 | tf_op jit(solution)/shard_map/while/body/eval_jaxpr/all_gather | solution.py:152
  560.0 22.5 %all-gather.27.cloned.1.call-done = bf16[512,1024]{1,0:T(8,128)(2,1)} async-done(((bf16[256,1024]{1,0:T(8,128)(2,1)}), bf16[512,1024]{1,0:T(8,128)(2,1)}) %all-gather.27.cloned.1.call-update) | async-done | bytes 1048592 | tf_op jit(solution)/shard_map/while/body/eval_jaxpr/all_gather | solution.py:187
  612.9 10.9 reduce-scatter.39.cloned.1.call-done
  627.8 21.4 %all_gather.91 = bf16[2,8,64]{1,0,2:T(2,128)(2,1)S(1)} all-gather(bf16[2,8,4]{1,0,2:T(2,128)(2,1)S(1)} %get-tuple-element.827), channel_id=1, replica_groups=mesh['dp'=16,'tensor'=2] {'dp'}, dimensions={2}, use_global_device_ids=true | all-gather | bytes 2176 | tf_op jit(solution)/shard_map/while/body/eval_jaxpr/all_gather | solution.py:110
  650.5 47.3 %all-gather.17.cloned.1.call-done = bf16[3,1024,512]{2,1,0:T(8,128)(2,1)} async-done(((bf16[3,64,512]{2,1,0:T(8,128)(2,1)}), bf16[3,1024,512]{2,1,0:T(8,128)(2,1)}) %all-gather.17.cloned.1.call-update) | async-done | bytes 3145744 | tf_op jit(solution)/shard_map/while/body/eval_jaxpr/all_gather | solution.py:109
  711.4 18.6 %reduce-scatter.33.cloned.1.call-done = bf16[256,1024]{1,0:T(8,128)(2,1)} async-done(((bf16[512,1024]{1,0:T(8,128)(2,1)}), bf16[256,1024]{1,0:T(8,128)(2,1)}) %reduce-scatter.33.cloned.1.call-update) | async-done | bytes 524304 | tf_op jit(solution)/shard_map/while/body/eval_jaxpr/reduce_scatter | solution.py:128
  735.5 21.5 %all_gather.89 = bf16[1,2048]{1,0:T(2,128)(2,1)S(1)} all-gather(bf16[1,128]{1,0:T(2,128)(2,1)S(1)} %get-tuple-element.832), channel_id=1, replica_groups=mesh['dp'=16,'tensor'=2] {'dp'}, dimensions={1}, use_global_device_ids=true | all-gather | bytes 4352 | tf_op jit(solution)/shard_map/while/body/eval_jaxpr/all_gather | solution.py:113
  757.0 25.9 %all-gather.21.cloned.1.call-done = bf16[1024,2048]{1,0:T(8,128)(2,1)} async-done(((bf16[64,2048]{1,0:T(8,128)(2,1)}), bf16[1024,2048]{1,0:T(8,128)(2,1)}) %all-gather.21.cloned.1.call-update) | async-done | bytes 4194320 | tf_op jit(solution)/shard_map/while/body/eval_jaxpr/all_gather | solution.py:112
  782.9 21.9 %all-gather.19.cloned.1.call-done = bf16[512,1024]{1,0:T(8,128)(2,1)} async-done(((bf16[256,1024]{1,0:T(8,128)(2,1)}), bf16[512,1024]{1,0:T(8,128)(2,1)}) %all-gather.19.cloned.1.call-update) | async-done | bytes 1048592 | tf_op jit(solution)/shard_map/while/body/eval_jaxpr/all_gather | solution.py:136
  804.8 15.2 multiply_convert_fusion.4
  820.0 37.8 %all-gather.23.cloned.1.call-done = bf16[2048,1024]{0,1:T(8,128)(2,1)} async-done(((bf16[2048,64]{0,1:T(8,128)(2,1)}), bf16[2048,1024]{0,1:T(8,128)(2,1)}) %all-gather.23.cloned.1.call-update) | async-done | bytes 4194320 | tf_op jit(solution)/shard_map/while/body/eval_jaxpr/all_gather | solution.py:114
  857.8 6.2 convolution_convert_fusion.9
  864.0 18.9 %reduce-scatter.35.cloned.1.call-done = bf16[256,1024]{1,0:T(8,128)(2,1)} async-done(((bf16[512,1024]{1,0:T(8,128)(2,1)}), bf16[256,1024]{1,0:T(8,128)(2,1)}) %reduce-scatter.35.cloned.1.call-update) | async-done | bytes 524304 | tf_op jit(solution)/shard_map/while/body/eval_jaxpr/reduce_scatter | solution.py:141
  889.2 21.2 %all-gather.25.cloned.1.call-done = bf16[512,1024]{1,0:T(8,128)(2,1)} async-done(((bf16[256,1024]{1,0:T(8,128)(2,1)}), bf16[512,1024]{1,0:T(8,128)(2,1)}) %all-gather.25.cloned.1.call-update) | async-done | bytes 1048592 | tf_op jit(solution)/shard_map/while/body/eval_jaxpr/all_gather | solution.py:162
  910.4 8.7 convert_reduce_fusion.6
  927.0 17.5 %reduce-scatter.37.cloned.1.call-done = bf16[256,1024]{1,0:T(8,128)(2,1)} async-done(((bf16[512,1024]{1,0:T(8,128)(2,1)}), bf16[256,1024]{1,0:T(8,128)(2,1)}) %reduce-scatter.37.cloned.1.call-update) | async-done | bytes 524304 | tf_op jit(solution)/shard_map/while/body/eval_jaxpr/reduce_scatter | solution.py:175
  949.7 10.1 select_add_fusion.11
  959.8 9.0 select_add_fusion.10
  968.9 15.9 all-gather.29.cloned.1.call-done
  984.8 22.5 %all-gather.27.cloned.1.call-done = bf16[512,1024]{1,0:T(8,128)(2,1)} async-done(((bf16[256,1024]{1,0:T(8,128)(2,1)}), bf16[512,1024]{1,0:T(8,128)(2,1)}) %all-gather.27.cloned.1.call-update) | async-done | bytes 1048592 | tf_op jit(solution)/shard_map/while/body/eval_jaxpr/all_gather | solution.py:187
  1034.1 7.4 bitcast_add_fusion.2
  1041.5 7.3 reduce-scatter.39.cloned.1.call-done
  1070.2 7.4 copy.68
  1079.6 61.4 %all-reduce = bf16[2,8,64]{1,2,0:T(8,128)(2,1)S(1)} all-reduce(bf16[2,8,64]{1,2,0:T(8,128)(2,1)S(1)} %copy.66), channel_id=8, replica_groups=mesh['dp'=16,'tensor'=2] {'dp'}, use_global_device_ids=true, to_apply=%region_26.27.clone | all-reduce | flops 1024 | bytes 4096
  1143.0 106.6 %reduce-scatter.29.cloned.1.call-done = f32[32,2]{1,0:T(8,128)} async-done(((f32[1024,2]{1,0:T(8,128)}), f32[32,2]{1,0:T(8,128)}) %reduce-scatter.29.cloned.1.call-update) | async-done | bytes 272
  1250.9 130.3 %reduce-scatter.31.cloned.1.call-done = f32[32,4]{1,0:T(8,128)} async-done(((f32[1024,4]{1,0:T(8,128)}), f32[32,4]{1,0:T(8,128)}) %reduce-scatter.31.cloned.1.call-update) | async-done | bytes 528
  1382.6 56.1 %reduce-scatter.21.cloned.1.call-done = bf16[512,64]{0,1:T(8,128)(2,1)} async-done(((bf16[512,1024]{0,1:T(8,128)(2,1)}), bf16[512,64]{0,1:T(8,128)(2,1)}) %reduce-scatter.21.cloned.1.call-update) | async-done | bytes 65552 | tf_op jit(solution)/shard_map/reduce_scatter | solution.py:253
  1440.2 67.5 %reduce-scatter.19.cloned.1.call-done = bf16[3,64,512]{2,1,0:T(8,128)(2,1)} async-done(((bf16[3,1024,512]{2,1,0:T(8,128)(2,1)}), bf16[3,64,512]{2,1,0:T(8,128)(2,1)}) %reduce-scatter.19.cloned.1.call-update) | async-done | bytes 196624 | tf_op jit(solution)/shard_map/reduce_scatter | solution.py:247
  1509.4 73.3 %reduce-scatter.23.cloned.1.call-done = bf16[64,2048]{1,0:T(8,128)(2,1)} async-done(((bf16[1024,2048]{1,0:T(8,128)(2,1)}), bf16[64,2048]{1,0:T(8,128)(2,1)}) %reduce-scatter.23.cloned.1.call-update) | async-done | bytes 262160 | tf_op jit(solution)/shard_map/reduce_scatter | solution.py:256
  1584.5 73.8 %reduce-scatter.25.cloned.1.call-done = bf16[2048,64]{0,1:T(8,128)(2,1)} async-done(((bf16[2048,1024]{0,1:T(8,128)(2,1)}), bf16[2048,64]{0,1:T(8,128)(2,1)}) %reduce-scatter.25.cloned.1.call-update) | async-done | bytes 262160 | tf_op jit(solution)/shard_map/reduce_scatter | solution.py:262
  (328 shorter events, 232.8 us)
Async XLA Ops:
  8.0 195.2 %copy-start.19 = (bf16[1,128]{1,0:T(2,128)(2,1)S(1)}, bf16[1,128]{1,0:T(2,128)(2,1)}, u32[]{:S(2)}) copy-start(bf16[1,128]{1,0:T(2,128)(2,1)} %param.19) | copy-start | bytes 772
  8.0 195.2 %copy-start.18 = (s32[2,512]{1,0:T(2,128)S(1)}, s32[2,512]{1,0:T(2,128)}, u32[]{:S(2)}) copy-start(s32[2,512]{1,0:T(2,128)} %param.14) | copy-start | bytes 12292
  9.1 8.2 collective-permute-start
  9.6 7.7 collective-permute-start.8
  17.3 7.1 collective-permute-start.1
  17.3 7.1 collective-permute-start.9
  24.4 7.2 collective-permute-start.2
  24.4 7.2 collective-permute-start.10
  31.6 7.2 collective-permute-start.3
  31.6 7.2 collective-permute-start.11
  38.8 7.2 collective-permute-start.4
  38.8 7.2 collective-permute-start.12
  46.0 7.2 collective-permute-start.5
  46.0 7.2 collective-permute-start.13
  53.2 7.1 collective-permute-start.6
  53.2 141.4 %collective-permute-start.14 = (bf16[512,64]{1,0:T(8,128)(2,1)S(1)}, bf16[512,64]{1,0:T(8,128)(2,1)S(1)}, u32[]{:S(2)}, u32[]{:S(2)}) collective-permute-start(bf16[512,64]{1,0:T(8,128)(2,1)S(1)} %collective-permute-done.13), channel_id=1, source_target_pairs={{0,30},{2,0},{4,2},{6,4},{8,6},{10,8},{12,10},{14,12},{16,14},{18,... | collective-permute-start | bytes 196616 | tf_op jit(solution)/shard_map/while/body/eval_jaxpr/ppermute | solution.py:22
  60.3 134.3 %collective-permute-start.7 = (bf16[512,64]{1,0:T(8,128)(2,1)S(1)}, bf16[512,64]{1,0:T(8,128)(2,1)S(1)}, u32[]{:S(2)}, u32[]{:S(2)}) collective-permute-start(bf16[512,64]{1,0:T(8,128)(2,1)S(1)} %collective-permute-done.6), channel_id=1, source_target_pairs={{0,2},{2,4},{4,6},{6,8},{8,10},{10,12},{12,14},{14,16},{16,18},{18... | collective-permute-start | bytes 196616 | tf_op jit(solution)/shard_map/while/body/eval_jaxpr/ppermute | solution.py:19
  203.6 22.3 %all-gather.15.cloned.1.call-start = ((), (), s32[]{:S(2)}) async-start(), calls=%async_computation.18 | async-start | bytes 1572864 | tf_op jit(solution)/shard_map/while/body/eval_jaxpr/all_gather | solution.py:116
  204.5 68.8 %all-gather.17.cloned.1.call-start = ((), (), s32[]{:S(2)}) async-start(), calls=%async_computation.19 | async-start | bytes 3342336 | tf_op jit(solution)/shard_map/while/body/eval_jaxpr/all_gather | solution.py:109
  205.3 100.3 %reduce-scatter.33.cloned.1.call-start = ((), (), s32[]{:S(2)}) async-start(), calls=%async_computation.20 | async-start | bytes 1572864 | tf_op jit(solution)/shard_map/while/body/eval_jaxpr/reduce_scatter | solution.py:128
  286.3 72.1 %all-gather.21.cloned.1.call-start = ((), (), s32[]{:S(2)}) async-start(), calls=%async_computation.22 | async-start | bytes 4456448 | tf_op jit(solution)/shard_map/while/body/eval_jaxpr/all_gather | solution.py:112
  286.9 93.4 %all-gather.19.cloned.1.call-start = ((), (), s32[]{:S(2)}) async-start(), calls=%async_computation.21 | async-start | bytes 1572864 | tf_op jit(solution)/shard_map/while/body/eval_jaxpr/all_gather | solution.py:136
  310.4 122.7 %all-gather.23.cloned.1.call-start = ((), (), s32[]{:S(2)}) async-start(), calls=%async_computation.23 | async-start | bytes 4456448 | tf_op jit(solution)/shard_map/while/body/eval_jaxpr/all_gather | solution.py:114
  311.0 147.3 %reduce-scatter.35.cloned.1.call-start = ((), (), s32[]{:S(2)}) async-start(), calls=%async_computation.24 | async-start | bytes 1572864 | tf_op jit(solution)/shard_map/while/body/eval_jaxpr/reduce_scatter | solution.py:141
  439.3 46.5 %all-gather.25.cloned.1.call-start = ((), (), s32[]{:S(2)}) async-start(), calls=%async_computation.25 | async-start | bytes 1572864 | tf_op jit(solution)/shard_map/while/body/eval_jaxpr/all_gather | solution.py:162
  464.3 55.5 %reduce-scatter.37.cloned.1.call-start = ((), (), s32[]{:S(2)}) async-start(), calls=%async_computation.26 | async-start | bytes 1572864 | tf_op jit(solution)/shard_map/while/body/eval_jaxpr/reduce_scatter | solution.py:175
  499.3 60.7 %all-gather.29.cloned.1.call-start = ((), (), s32[]{:S(2)}) async-start(), calls=%async_computation.28 | async-start | bytes 1114112 | tf_op jit(solution)/shard_map/while/body/eval_jaxpr/all_gather | solution.py:152
  499.9 82.6 %all-gather.27.cloned.1.call-start = ((), (), s32[]{:S(2)}) async-start(), calls=%async_computation.27 | async-start | bytes 1572864 | tf_op jit(solution)/shard_map/while/body/eval_jaxpr/all_gather | solution.py:187
  524.7 99.1 %reduce-scatter.39.cloned.1.call-start = ((), (), s32[]{:S(2)}) async-start(), calls=%async_computation.29 | async-start | bytes 1572864 | tf_op jit(solution)/shard_map/while/body/eval_jaxpr/reduce_scatter | solution.py:209
  626.2 24.3 %all-gather.15.cloned.1.call-start = ((), (), s32[]{:S(2)}) async-start(), calls=%async_computation.18 | async-start | bytes 1572864 | tf_op jit(solution)/shard_map/while/body/eval_jaxpr/all_gather | solution.py:116
  627.1 70.7 %all-gather.17.cloned.1.call-start = ((), (), s32[]{:S(2)}) async-start(), calls=%async_computation.19 | async-start | bytes 3342336 | tf_op jit(solution)/shard_map/while/body/eval_jaxpr/all_gather | solution.py:109
  627.7 102.3 %reduce-scatter.33.cloned.1.call-start = ((), (), s32[]{:S(2)}) async-start(), calls=%async_computation.20 | async-start | bytes 1572864 | tf_op jit(solution)/shard_map/while/body/eval_jaxpr/reduce_scatter | solution.py:128
  710.7 72.1 %all-gather.21.cloned.1.call-start = ((), (), s32[]{:S(2)}) async-start(), calls=%async_computation.22 | async-start | bytes 4456448 | tf_op jit(solution)/shard_map/while/body/eval_jaxpr/all_gather | solution.py:112
  711.3 93.4 %all-gather.19.cloned.1.call-start = ((), (), s32[]{:S(2)}) async-start(), calls=%async_computation.21 | async-start | bytes 1572864 | tf_op jit(solution)/shard_map/while/body/eval_jaxpr/all_gather | solution.py:136
  734.9 122.9 %all-gather.23.cloned.1.call-start = ((), (), s32[]{:S(2)}) async-start(), calls=%async_computation.23 | async-start | bytes 4456448 | tf_op jit(solution)/shard_map/while/body/eval_jaxpr/all_gather | solution.py:114
  735.5 147.5 %reduce-scatter.35.cloned.1.call-start = ((), (), s32[]{:S(2)}) async-start(), calls=%async_computation.24 | async-start | bytes 1572864 | tf_op jit(solution)/shard_map/while/body/eval_jaxpr/reduce_scatter | solution.py:141
  864.0 46.5 %all-gather.25.cloned.1.call-start = ((), (), s32[]{:S(2)}) async-start(), calls=%async_computation.25 | async-start | bytes 1572864 | tf_op jit(solution)/shard_map/while/body/eval_jaxpr/all_gather | solution.py:162
  889.0 55.5 %reduce-scatter.37.cloned.1.call-start = ((), (), s32[]{:S(2)}) async-start(), calls=%async_computation.26 | async-start | bytes 1572864 | tf_op jit(solution)/shard_map/while/body/eval_jaxpr/reduce_scatter | solution.py:175
  924.0 60.8 %all-gather.29.cloned.1.call-start = ((), (), s32[]{:S(2)}) async-start(), calls=%async_computation.28 | async-start | bytes 1114112 | tf_op jit(solution)/shard_map/while/body/eval_jaxpr/all_gather | solution.py:152
  924.7 82.5 %all-gather.27.cloned.1.call-start = ((), (), s32[]{:S(2)}) async-start(), calls=%async_computation.27 | async-start | bytes 1572864 | tf_op jit(solution)/shard_map/while/body/eval_jaxpr/all_gather | solution.py:187
  949.3 99.5 %reduce-scatter.39.cloned.1.call-start = ((), (), s32[]{:S(2)}) async-start(), calls=%async_computation.29 | async-start | bytes 1572864 | tf_op jit(solution)/shard_map/while/body/eval_jaxpr/reduce_scatter | solution.py:209
  1053.7 87.9 %reduce-scatter.27.cloned.1.call-start = ((), (), s32[]{:S(2)}) async-start(), calls=%async_computation.15 | async-start | bytes 557056
  1054.9 194.7 %reduce-scatter.29.cloned.1.call-start = ((), (), s32[]{:S(2)}) async-start(), calls=%async_computation.16 | async-start | bytes 540672
  1056.0 325.3 %reduce-scatter.31.cloned.1.call-start = ((), (), s32[]{:S(2)}) async-start(), calls=%async_computation.17 | async-start | bytes 540672
  1057.1 381.6 %reduce-scatter.21.cloned.1.call-start = ((), (), s32[]{:S(2)}) async-start(), calls=%async_computation.12 | async-start | bytes 1114112 | tf_op jit(solution)/shard_map/reduce_scatter | solution.py:253
  1058.6 449.2 %reduce-scatter.19.cloned.1.call-start = ((), (), s32[]{:S(2)}) async-start(), calls=%async_computation.11 | async-start | bytes 3342336 | tf_op jit(solution)/shard_map/reduce_scatter | solution.py:247
  1064.0 518.7 %reduce-scatter.23.cloned.1.call-start = ((), (), s32[]{:S(2)}) async-start(), calls=%async_computation.13 | async-start | bytes 4456448 | tf_op jit(solution)/shard_map/reduce_scatter | solution.py:256
  1070.2 588.2 %reduce-scatter.25.cloned.1.call-start = ((), (), s32[]{:S(2)}) async-start(), calls=%async_computation.14 | async-start | bytes 4456448 | tf_op jit(solution)/shard_map/reduce_scatter | solution.py:262
  (43 other events, 460.6 us)
Sparse Core Ops, SparseCore 0:
  206.6 19.2 all-gather.14
  228.1 45.1 all-gather.16
  286.4 19.1 reduce-scatter.32
  307.8 50.5 all-gather.20
  360.4 19.7 all-gather.18
  382.5 50.5 all-gather.22
  439.5 18.7 reduce-scatter.34
  464.4 21.3 all-gather.24
  499.5 20.3 reduce-scatter.36
  522.0 37.9 all-gather.28
  562.2 20.2 all-gather.26
  603.4 20.3 reduce-scatter.38
  629.2 21.2 all-gather.14
  652.6 45.1 all-gather.16
  710.9 19.1 reduce-scatter.32
  732.3 50.5 all-gather.20
  784.9 19.7 all-gather.18
  807.0 50.7 all-gather.22
  864.1 18.7 reduce-scatter.34
  889.1 21.3 all-gather.24
  924.1 20.3 reduce-scatter.36
  946.8 37.9 all-gather.28
  987.0 20.2 all-gather.26
  1028.5 20.3 reduce-scatter.38
Sparse Core Ops, SparseCore 1:
  1058.3 55.8 reduce-scatter.26
  1116.9 132.6 reduce-scatter.28
  1251.7 129.5 reduce-scatter.30
  1385.3 53.3 reduce-scatter.20
  1442.6 65.1 reduce-scatter.18
  1511.6 71.1 reduce-scatter.22
  1587.0 71.3 reduce-scatter.24
